TPU v7x, 128 devices: a whole 4x4x4 slice. The times are simulated.
128 devices in a mesh: leaf: 8 (over x, core), prow: 4 (over z), pcol: 4 (over y).
Axes of the slice: x: 4, y: 4, z: 4, core: 2. Of those that a mesh axis runs over, the one named last changes fastest.
Arguments:
- subtree_factor: float32 [8, 2, 8, 256, 2048], P('leaf', None, None, 'prow', 'pcol'), may hold values from -0.09375 to 0.09375
- sub_linv: float32 [8, 2, 8, 256, 256], P('leaf', None, None, 'prow'), may hold values from -0.05 to 1.05
- sub_uinv: float32 [8, 2, 8, 256, 256], P('leaf', None, None, 'prow'), may hold values from -0.05 to 1.05
- lower_panel: float32 [8, 4, 256, 2, 2048], P('leaf', None, 'prow', None, 'pcol'), may hold values from -0.0234375 to 0.0234375
- upper_panel: float32 [8, 2, 8, 256, 1024], P('leaf', None, None, 'prow', 'pcol'), may hold values from -0.125 to 0.125
- panel_rows: int32 [8, 4, 2], P('leaf'), may hold values 0 or 1
- upper_level_factor: float32 [4, 256, 1024], P(None, 'prow', 'pcol'), may hold values from -0.125 to 0.125
- top_linv: float32 [4, 256, 256], P(None, 'prow'), may hold values from -0.05 to 1.05
- top_uinv: float32 [4, 256, 256], P(None, 'prow'), may hold values from -0.05 to 1.05
- sub_rhs: float32 [8, 2, 8, 256, 256], P('leaf', None, None, 'prow'), may hold values from -6 to 6
- top_rhs: float32 [4, 256, 256], P(None, 'prow', 'leaf'), may hold values from -6 to 6
Outputs:
- sub_solution: float32 [8, 2, 8, 256, 256], P('leaf', None, 'pcol')
- top_solution: float32 [4, 256, 256], P('pcol', None, 'leaf')
All inputs are finite; a program needn't handle non-finite values. No bound on the sum of `panel_rows` on one device may be relied on, other than what follows from the above.
Results may differ from a plain program's by a relative error of at most 0.00013.
Values sent between devices are 32-bit elements; how exact they have to be, the bound alone decides.
A program may use at most 128 MiB of HBM per device.

v0:
```python
import jax
import jax.numpy as jnp
from jax import lax
from jax.sharding import PartitionSpec as P

TOP_PRECISION = lax.Precision.HIGHEST


def block_order(block_count, forward):
    return range(block_count) if forward else range(block_count - 1, -1, -1)


def sweep_blocks(factor_row_block, inverses, right_side, coupling, owned_start, my_col, forward):
    groups, block_count, tile_rows, columns = right_side.shape
    block_rows = inverses.shape[3]
    owned_count = factor_row_block.shape[3] // block_rows
    solved = jnp.zeros((groups, block_count, block_rows, columns), jnp.float32)
    for sweep_step_index in block_order(block_count, forward):
        held_value_entries = lax.dynamic_slice_in_dim(solved, owned_start, owned_count, 1)
        held_value_entries = held_value_entries.reshape(groups, owned_count * block_rows, columns)
        partial_value = coupling[:, sweep_step_index] + jnp.einsum(
            "pht,ptj->phj",
            factor_row_block[:, sweep_step_index],
            held_value_entries,
            precision=TOP_PRECISION,
        )
        local_side = jnp.where(my_col == 0, right_side[:, sweep_step_index], 0.0) - partial_value
        inverse_part = jnp.einsum(
            "gab,gar->gbr", inverses[:, sweep_step_index], local_side, precision=TOP_PRECISION
        )
        block_value = lax.psum(inverse_part, ("prow", "pcol"))
        solved = solved.at[:, sweep_step_index].set(block_value)
    return solved


def per_device(
    subtree_factor,
    sub_linv,
    sub_uinv,
    lower_panel,
    upper_panel,
    panel_rows,
    upper_level_factor,
    top_linv,
    top_uinv,
    sub_rhs,
    top_rhs,
):
    my_row = lax.axis_index("prow")
    my_col = lax.axis_index("pcol")
    block_rows = sub_linv.shape[4]
    tile_rows = sub_rhs.shape[3]
    groups = sub_rhs.shape[1]
    block_count = sub_rhs.shape[2]
    sub_owned = subtree_factor.shape[4] // block_rows
    top_owned = upper_level_factor.shape[2] // block_rows
    present = panel_rows[0].astype(jnp.float32)
    linv_rows, uinv_rows, top_linv_rows, top_uinv_rows = (sub_linv, sub_uinv, top_linv, top_uinv)
    lower_sub = sweep_blocks(
        subtree_factor[0],
        linv_rows[0],
        sub_rhs[0],
        jnp.zeros(sub_rhs[0].shape, jnp.float32),
        my_col * sub_owned,
        my_col,
        True,
    )
    lower_owned = lax.dynamic_slice_in_dim(lower_sub, my_col * sub_owned, sub_owned, 1)
    lower_owned = lower_owned.reshape(groups, sub_owned * block_rows, lower_sub.shape[3])
    contrib_part = jnp.einsum(
        "tasm,ts,smr->tar", lower_panel[0], present, lower_owned, precision=TOP_PRECISION
    )
    contrib = lax.psum(contrib_part, "leaf")
    upper_level_side = lax.all_gather(top_rhs, "leaf", axis=2, tiled=True)
    upper_level_lower = sweep_blocks(
        upper_level_factor[None],
        top_linv_rows[None],
        upper_level_side[None],
        contrib[None],
        my_col * top_owned,
        my_col,
        True,
    )
    top_rows = lax.dynamic_slice_in_dim(upper_level_lower, my_row * tile_rows, tile_rows, 2)
    top_upper = sweep_blocks(
        upper_level_factor[None],
        top_uinv_rows[None],
        top_rows,
        jnp.zeros(top_rows.shape, jnp.float32),
        my_col * top_owned,
        my_col,
        False,
    )[0]
    top_out = lax.dynamic_slice_in_dim(
        top_upper, lax.axis_index("leaf") * top_rhs.shape[2], top_rhs.shape[2], 2
    )
    top_out = lax.dynamic_slice_in_dim(top_out, my_col * top_owned, top_owned, 0)
    top_mine = lax.dynamic_slice_in_dim(top_upper, my_col * top_owned, top_owned, 0)
    mask_mine = lax.dynamic_slice_in_dim(present, my_col * top_owned, top_owned, 0)
    upper_local = upper_panel[0].reshape(groups, block_count, tile_rows, top_owned, block_rows)
    coupling = jnp.einsum(
        "skatb,ts,tbr->skar", upper_local, mask_mine, top_mine, precision=TOP_PRECISION
    )
    sub_rows = lax.dynamic_slice_in_dim(lower_sub, my_row * tile_rows, tile_rows, 2)
    upper_sub = sweep_blocks(
        subtree_factor[0], uinv_rows[0], sub_rows, coupling, my_col * sub_owned, my_col, False
    )
    sub_out = lax.dynamic_slice_in_dim(upper_sub, my_col * sub_owned, sub_owned, 1)
    return (sub_out[None], top_out)


def solution(mesh):
    placed = (
        P("leaf", None, None, "prow", "pcol"),
        P("leaf", None, None, "prow", None),
        P("leaf", None, None, "prow", None),
        P("leaf", None, "prow", None, "pcol"),
        P("leaf", None, None, "prow", "pcol"),
        P("leaf", None, None),
        P(None, "prow", "pcol"),
        P(None, "prow", None),
        P(None, "prow", None),
        P("leaf", None, None, "prow", None),
        P(None, "prow", "leaf"),
    )
    return jax.shard_map(
        per_device,
        mesh=mesh,
        in_specs=placed,
        out_specs=(P("leaf", None, "pcol", None, None), P("pcol", None, "leaf")),
        check_vma=False,
    )
```

profile of v0, /device:TPU:0, one launch (start us, length us, event | category | flops | bytes accessed | tf_op | source)
XLA Modules:
  0.0 2303.5 jit_solution(17855429060302195027)
XLA Ops:
  15.9 88.4 %all-reduce.30.cloned.1.call-done = f32[2,1,256,256]{3,2,0,1:T(8,128)} async-done(((f32[2,1,256,256]{3,2,0,1:T(8,128)}), f32[2,1,256,256]{3,2,0,1:T(8,128)}) %all-reduce.30.cloned.1.call-update) | async-done | bytes 524304 | tf_op jit(solution)/shard_map/psum | solution.py:31
  113.0 80.7 %all-reduce.32.cloned.1.call-done = f32[2,1,256,256]{3,2,0,1:T(8,128)} async-done(((f32[2,1,256,256]{3,2,0,1:T(8,128)}), f32[2,1,256,256]{3,2,0,1:T(8,128)}) %all-reduce.32.cloned.1.call-update) | async-done | bytes 524304 | tf_op jit(solution)/shard_map/psum | solution.py:31
  201.2 85.3 %all-reduce.34.cloned.1.call-done = f32[2,1,256,256]{3,2,0,1:T(8,128)} async-done(((f32[2,1,256,256]{3,2,0,1:T(8,128)}), f32[2,1,256,256]{3,2,0,1:T(8,128)}) %all-reduce.34.cloned.1.call-update) | async-done | bytes 524304 | tf_op jit(solution)/shard_map/psum | solution.py:31
  293.9 85.3 %all-reduce.36.cloned.1.call-done = f32[2,1,256,256]{3,2,0,1:T(8,128)} async-done(((f32[2,1,256,256]{3,2,0,1:T(8,128)}), f32[2,1,256,256]{3,2,0,1:T(8,128)}) %all-reduce.36.cloned.1.call-update) | async-done | bytes 524304 | tf_op jit(solution)/shard_map/psum | solution.py:31
  386.6 85.3 %all-reduce.38.cloned.1.call-done = f32[2,1,256,256]{3,2,0,1:T(8,128)} async-done(((f32[2,1,256,256]{3,2,0,1:T(8,128)}), f32[2,1,256,256]{3,2,0,1:T(8,128)}) %all-reduce.38.cloned.1.call-update) | async-done | bytes 524304 | tf_op jit(solution)/shard_map/psum | solution.py:31
  479.3 85.2 %all-reduce.40.cloned.1.call-done = f32[2,1,256,256]{3,2,0,1:T(8,128)} async-done(((f32[2,1,256,256]{3,2,0,1:T(8,128)}), f32[2,1,256,256]{3,2,0,1:T(8,128)}) %all-reduce.40.cloned.1.call-update) | async-done | bytes 524304 | tf_op jit(solution)/shard_map/psum | solution.py:31
  572.0 85.3 %all-reduce.42.cloned.1.call-done = f32[2,1,256,256]{3,2,0,1:T(8,128)} async-done(((f32[2,1,256,256]{3,2,0,1:T(8,128)}), f32[2,1,256,256]{3,2,0,1:T(8,128)}) %all-reduce.42.cloned.1.call-update) | async-done | bytes 524304 | tf_op jit(solution)/shard_map/psum | solution.py:31
  667.6 82.2 %all-reduce.44.cloned.1.call-done = f32[2,1,256,256]{3,2,0,1:T(8,128)} async-done(((f32[2,1,256,256]{3,2,0,1:T(8,128)}), f32[2,1,256,256]{3,2,0,1:T(8,128)}) %all-reduce.44.cloned.1.call-update) | async-done | bytes 524304 | tf_op jit(solution)/shard_map/psum | solution.py:31
  816.8 85.7 %all-reduce.48.cloned.1.call-done = f32[1,1,256,256]{3,2,1,0:T(8,128)} async-done(((f32[1,1,256,256]{3,2,1,0:T(8,128)}), f32[1,1,256,256]{3,2,1,0:T(8,128)}) %all-reduce.48.cloned.1.call-update) | async-done | bytes 262160 | tf_op jit(solution)/shard_map/psum | solution.py:31
  907.9 82.4 %all-reduce.50.cloned.1.call-done = f32[1,1,256,256]{3,2,1,0:T(8,128)} async-done(((f32[1,1,256,256]{3,2,1,0:T(8,128)}), f32[1,1,256,256]{3,2,1,0:T(8,128)}) %all-reduce.50.cloned.1.call-update) | async-done | bytes 262160 | tf_op jit(solution)/shard_map/psum | solution.py:31
  995.2 84.5 %all-reduce.52.cloned.1.call-done = f32[1,1,256,256]{3,2,1,0:T(8,128)} async-done(((f32[1,1,256,256]{3,2,1,0:T(8,128)}), f32[1,1,256,256]{3,2,1,0:T(8,128)}) %all-reduce.52.cloned.1.call-update) | async-done | bytes 262160 | tf_op jit(solution)/shard_map/psum | solution.py:31
  1084.7 84.5 %all-reduce.54.cloned.1.call-done = f32[1,1,256,256]{3,2,1,0:T(8,128)} async-done(((f32[1,1,256,256]{3,2,1,0:T(8,128)}), f32[1,1,256,256]{3,2,1,0:T(8,128)}) %all-reduce.54.cloned.1.call-update) | async-done | bytes 262160 | tf_op jit(solution)/shard_map/psum | solution.py:31
  1173.0 84.5 %all-reduce.56.cloned.1.call-done = f32[1,1,256,256]{2,3,1,0:T(8,128)} async-done(((f32[1,1,256,256]{2,3,1,0:T(8,128)}), f32[1,1,256,256]{2,3,1,0:T(8,128)}) %all-reduce.56.cloned.1.call-update) | async-done | bytes 262160 | tf_op jit(solution)/shard_map/psum | solution.py:31
  1262.8 82.5 %all-reduce.58.cloned.1.call-done = f32[1,1,256,256]{2,3,1,0:T(8,128)} async-done(((f32[1,1,256,256]{2,3,1,0:T(8,128)}), f32[1,1,256,256]{2,3,1,0:T(8,128)}) %all-reduce.58.cloned.1.call-update) | async-done | bytes 262160 | tf_op jit(solution)/shard_map/psum | solution.py:31
  1350.3 84.5 %all-reduce.60.cloned.1.call-done = f32[1,1,256,256]{2,3,1,0:T(8,128)} async-done(((f32[1,1,256,256]{2,3,1,0:T(8,128)}), f32[1,1,256,256]{2,3,1,0:T(8,128)}) %all-reduce.60.cloned.1.call-update) | async-done | bytes 262160 | tf_op jit(solution)/shard_map/psum | solution.py:31
  1442.3 82.0 %all-reduce.62.cloned.1.call-done = f32[1,256,256]{1,2,0:T(8,128)} async-done(((f32[1,256,256]{1,2,0:T(8,128)}), f32[1,256,256]{1,2,0:T(8,128)}) %all-reduce.62.cloned.1.call-update) | async-done | bytes 262160 | tf_op jit(solution)/shard_map/psum | solution.py:31
  1534.6 85.1 %all-reduce.64.cloned.1.call-done = f32[2,1,256,256]{2,3,0,1:T(8,128)} async-done(((f32[2,1,256,256]{2,3,0,1:T(8,128)}), f32[2,1,256,256]{2,3,0,1:T(8,128)}) %all-reduce.64.cloned.1.call-update) | async-done | bytes 524304 | tf_op jit(solution)/shard_map/psum | solution.py:31
  1632.5 81.6 %all-reduce.66.cloned.1.call-done = f32[2,1,256,256]{2,3,0,1:T(8,128)} async-done(((f32[2,1,256,256]{2,3,0,1:T(8,128)}), f32[2,1,256,256]{2,3,0,1:T(8,128)}) %all-reduce.66.cloned.1.call-update) | async-done | bytes 524304 | tf_op jit(solution)/shard_map/psum | solution.py:31
  1725.3 85.2 %all-reduce.68.cloned.1.call-done = f32[2,1,256,256]{2,3,0,1:T(8,128)} async-done(((f32[2,1,256,256]{2,3,0,1:T(8,128)}), f32[2,1,256,256]{2,3,0,1:T(8,128)}) %all-reduce.68.cloned.1.call-update) | async-done | bytes 524304 | tf_op jit(solution)/shard_map/psum | solution.py:31
  1821.7 85.2 %all-reduce.70.cloned.1.call-done = f32[2,1,256,256]{2,3,0,1:T(8,128)} async-done(((f32[2,1,256,256]{2,3,0,1:T(8,128)}), f32[2,1,256,256]{2,3,0,1:T(8,128)}) %all-reduce.70.cloned.1.call-update) | async-done | bytes 524304 | tf_op jit(solution)/shard_map/psum | solution.py:31
  1918.0 85.2 %all-reduce.72.cloned.1.call-done = f32[2,1,256,256]{2,3,0,1:T(8,128)} async-done(((f32[2,1,256,256]{2,3,0,1:T(8,128)}), f32[2,1,256,256]{2,3,0,1:T(8,128)}) %all-reduce.72.cloned.1.call-update) | async-done | bytes 524304 | tf_op jit(solution)/shard_map/psum | solution.py:31
  2014.4 85.3 %all-reduce.74.cloned.1.call-done = f32[2,1,256,256]{2,3,0,1:T(8,128)} async-done(((f32[2,1,256,256]{2,3,0,1:T(8,128)}), f32[2,1,256,256]{2,3,0,1:T(8,128)}) %all-reduce.74.cloned.1.call-update) | async-done | bytes 524304 | tf_op jit(solution)/shard_map/psum | solution.py:31
  2110.9 85.2 %all-reduce.76.cloned.1.call-done = f32[2,1,256,256]{2,3,0,1:T(8,128)} async-done(((f32[2,1,256,256]{2,3,0,1:T(8,128)}), f32[2,1,256,256]{2,3,0,1:T(8,128)}) %all-reduce.76.cloned.1.call-update) | async-done | bytes 524304 | tf_op jit(solution)/shard_map/psum | solution.py:31
  2208.7 83.8 %all-reduce.78.cloned.1.call-done = f32[2,1,256,256]{2,3,0,1:T(8,128)} async-done(((f32[2,1,256,256]{2,3,0,1:T(8,128)}), f32[2,1,256,256]{2,3,0,1:T(8,128)}) %all-reduce.78.cloned.1.call-update) | async-done | bytes 524304 | tf_op jit(solution)/shard_map/psum | solution.py:31
  (184 shorter events, 264.3 us)
Async XLA Ops:
  15.8 177.9 %all-reduce.32.cloned.1.call-start = ((), (), s32[]{:S(2)}) async-start(), calls=%async_computation.1 | async-start | bytes 1048576 | tf_op jit(solution)/shard_map/psum | solution.py:31
  109.6 176.9 %all-reduce.34.cloned.1.call-start = ((), (), s32[]{:S(2)}) async-start(), calls=%async_computation.2 | async-start | bytes 1048576 | tf_op jit(solution)/shard_map/psum | solution.py:31
  201.1 178.0 %all-reduce.36.cloned.1.call-start = ((), (), s32[]{:S(2)}) async-start(), calls=%async_computation.3 | async-start | bytes 1048576 | tf_op jit(solution)/shard_map/psum | solution.py:31
  293.9 178.0 %all-reduce.38.cloned.1.call-start = ((), (), s32[]{:S(2)}) async-start(), calls=%async_computation.4 | async-start | bytes 1048576 | tf_op jit(solution)/shard_map/psum | solution.py:31
  386.6 177.9 %all-reduce.40.cloned.1.call-start = ((), (), s32[]{:S(2)}) async-start(), calls=%async_computation.5 | async-start | bytes 1048576 | tf_op jit(solution)/shard_map/psum | solution.py:31
  479.3 177.9 %all-reduce.42.cloned.1.call-start = ((), (), s32[]{:S(2)}) async-start(), calls=%async_computation.6 | async-start | bytes 1048576 | tf_op jit(solution)/shard_map/psum | solution.py:31
  571.9 177.9 %all-reduce.44.cloned.1.call-start = ((), (), s32[]{:S(2)}) async-start(), calls=%async_computation.7 | async-start | bytes 1048576 | tf_op jit(solution)/shard_map/psum | solution.py:31
  664.6 150.2 %all-reduce.46.cloned.1.call-start = ((), (), s32[]{:S(2)}) async-start(), calls=%async_computation.8 | async-start | bytes 524288 | tf_op jit(solution)/shard_map/psum | solution.py:73
  755.0 147.5 %all-reduce.48.cloned.1.call-start = ((), (), s32[]{:S(2)}) async-start(), calls=%async_computation.9 | async-start | bytes 524288 | tf_op jit(solution)/shard_map/psum | solution.py:31
  816.8 173.4 %all-reduce.50.cloned.1.call-start = ((), (), s32[]{:S(2)}) async-start(), calls=%async_computation.10 | async-start | bytes 524288 | tf_op jit(solution)/shard_map/psum | solution.py:31
  905.8 173.9 %all-reduce.52.cloned.1.call-start = ((), (), s32[]{:S(2)}) async-start(), calls=%async_computation.11 | async-start | bytes 524288 | tf_op jit(solution)/shard_map/psum | solution.py:31
  995.1 174.0 %all-reduce.54.cloned.1.call-start = ((), (), s32[]{:S(2)}) async-start(), calls=%async_computation.12 | async-start | bytes 524288 | tf_op jit(solution)/shard_map/psum | solution.py:31
  1084.7 172.8 %all-reduce.56.cloned.1.call-start = ((), (), s32[]{:S(2)}) async-start(), calls=%async_computation.13 | async-start | bytes 524288 | tf_op jit(solution)/shard_map/psum | solution.py:31
  1172.9 172.3 %all-reduce.58.cloned.1.call-start = ((), (), s32[]{:S(2)}) async-start(), calls=%async_computation.14 | async-start | bytes 524288 | tf_op jit(solution)/shard_map/psum | solution.py:31
  1260.7 174.1 %all-reduce.60.cloned.1.call-start = ((), (), s32[]{:S(2)}) async-start(), calls=%async_computation.15 | async-start | bytes 524288 | tf_op jit(solution)/shard_map/psum | solution.py:31
  1350.2 174.0 %all-reduce.62.cloned.1.call-start = ((), (), s32[]{:S(2)}) async-start(), calls=%async_computation.16 | async-start | bytes 524288 | tf_op jit(solution)/shard_map/psum | solution.py:31
  1439.8 180.0 %all-reduce.64.cloned.1.call-start = ((), (), s32[]{:S(2)}) async-start(), calls=%async_computation.17 | async-start | bytes 1048576 | tf_op jit(solution)/shard_map/psum | solution.py:31
  1534.6 179.5 %all-reduce.66.cloned.1.call-start = ((), (), s32[]{:S(2)}) async-start(), calls=%async_computation.18 | async-start | bytes 1048576 | tf_op jit(solution)/shard_map/psum | solution.py:31
  1628.9 181.6 %all-reduce.68.cloned.1.call-start = ((), (), s32[]{:S(2)}) async-start(), calls=%async_computation.19 | async-start | bytes 1048576 | tf_op jit(solution)/shard_map/psum | solution.py:31
  1725.2 181.6 %all-reduce.70.cloned.1.call-start = ((), (), s32[]{:S(2)}) async-start(), calls=%async_computation.20 | async-start | bytes 1048576 | tf_op jit(solution)/shard_map/psum | solution.py:31
  1821.6 181.6 %all-reduce.72.cloned.1.call-start = ((), (), s32[]{:S(2)}) async-start(), calls=%async_computation.21 | async-start | bytes 1048576 | tf_op jit(solution)/shard_map/psum | solution.py:31
  1918.0 181.7 %all-reduce.74.cloned.1.call-start = ((), (), s32[]{:S(2)}) async-start(), calls=%async_computation.22 | async-start | bytes 1048576 | tf_op jit(solution)/shard_map/psum | solution.py:31
  2014.3 181.7 %all-reduce.76.cloned.1.call-start = ((), (), s32[]{:S(2)}) async-start(), calls=%async_computation.23 | async-start | bytes 1048576 | tf_op jit(solution)/shard_map/psum | solution.py:31
  2110.8 181.7 %all-reduce.78.cloned.1.call-start = ((), (), s32[]{:S(2)}) async-start(), calls=%async_computation.24 | async-start | bytes 1048576 | tf_op jit(solution)/shard_map/psum | solution.py:31
  (8 other events, 2078.1 us)
Sparse Core Ops, SparseCore 0:
  15.9 88.3 all-reduce.29
  109.7 84.0 all-reduce.31
  201.3 85.1 all-reduce.33
  294.0 85.1 all-reduce.35
  386.7 85.1 all-reduce.37
  479.4 85.0 all-reduce.39
  572.0 85.1 all-reduce.41
  664.7 85.0 all-reduce.43
  818.3 84.1 all-reduce.47
  905.9 84.2 all-reduce.49
  995.3 84.3 all-reduce.51
  1084.8 84.3 all-reduce.53
  1173.1 84.3 all-reduce.55
  1260.8 84.3 all-reduce.57
  1350.4 84.3 all-reduce.59
  1439.9 84.3 all-reduce.61
  1534.7 85.0 all-reduce.63
  1629.0 85.0 all-reduce.65
  1725.3 85.0 all-reduce.67
  1821.7 85.0 all-reduce.69
  1918.1 85.0 all-reduce.71
  2014.5 85.1 all-reduce.73
  2110.9 85.0 all-reduce.75
  2207.4 85.0 all-reduce.77
  (1 shorter events, 59.5 us)
where the time goes:
time: 2310 us; the launch traced here: 2300 us
  waiting for transfers between devices  2070 us (90%)
  local copies, waits for them, and re-layouts  108 us (5%)
  matrix products  93 us (4%)
    psum x24, waiting for transfers between devices, sweep_blocks(): block_value = lax.psum(inverse_part, ('prow', 'pcol'))  2020 us
    dot_general x24, matrix products, sweep_blocks(): jnp.einsum('gab,gar->gbr', inverses[:, sweep_step_index], local_side, pre...  53.3 us
    scatter x24, local copies, waits for them, and re-layouts, sweep_blocks(): solved = solved.at[:, sweep_step_index].set(block_value)  47.2 us
  transfers between devices with their start and end apart: 25, of which 25 were waited for; matrix products, arithmetic and copies ran while one was open for 1% of the time, Pallas kernels for 0%

commit v1 on v0

--- a/solution.py
+++ b/solution.py
@@ -28,7 +28,7 @@
         inverse_part = jnp.einsum(
             "gab,gar->gbr", inverses[:, sweep_step_index], local_side, precision=TOP_PRECISION
         )
-        block_value = lax.psum(inverse_part, ("prow", "pcol"))
+        block_value = lax.all_gather(inverse_part, ("prow", "pcol")).sum(axis=0)
         solved = solved.at[:, sweep_step_index].set(block_value)
     return solved
 

time: 2310 us -> 2020 us (0.87)
  waiting for transfers between devices: 2070 us -> 1610 us
  other arithmetic: 3.61 us -> 88.3 us
  local copies, waits for them, and re-layouts: 108 us -> 184 us
    psum x24 -> x0, waiting for transfers between devices: 2020 us -> none  [sweep_blocks(): block_value = lax.psum(inverse_part, ('prow', 'pcol'))]
    all_gather x0 -> x24, waiting for transfers between devices: none -> 1560 us  [sweep_blocks(): block_value = lax.all_gather(inverse_part, ('prow', 'pcol')).sum(axis=0)]
    reduce_sum x0 -> x24, other arithmetic: none -> 84.6 us  [sweep_blocks(): block_value = lax.all_gather(inverse_part, ('prow', 'pcol')).sum(axis=0)]
    unnamed x19 -> x37, local copies, waits for them, and re-layouts: 8.4 us -> 54.1 us
    dot_general x0 -> x16, local copies, waits for them, and re-layouts: none -> 31.7 us  [sweep_blocks(): jnp.einsum('gab,gar->gbr', inverses[:, sweep_step_index], local_side, pre...]
where the time goes in v1:
time: 2020 us; the launch traced here: 2000 us
  waiting for transfers between devices  1610 us (80%)
  local copies, waits for them, and re-layouts  184 us (9%)
  matrix products  91.8 us (5%)
  other arithmetic  88.3 us (4%)
    all_gather x24, waiting for transfers between devices, sweep_blocks(): block_value = lax.all_gather(inverse_part, ('prow', 'pcol')).sum(axis=0)  1560 us
    reduce_sum x24, other arithmetic, sweep_blocks(): block_value = lax.all_gather(inverse_part, ('prow', 'pcol')).sum(axis=0)  84.6 us
    unnamed x37, local copies, waits for them, and re-layouts  54.1 us
    dot_general x24, matrix products, sweep_blocks(): jnp.einsum('gab,gar->gbr', inverses[:, sweep_step_index], local_side, pre...  52.2 us
    dynamic_slice x28, local copies, waits for them, and re-layouts, sweep_blocks(): lax.dynamic_slice_in_dim(solved, owned_start, owned_count, 1)  43.5 us
    psum x1, waiting for transfers between devices, per_device(): contrib = lax.psum(contrib_part, 'leaf')  43 us
    scatter x24, local copies, waits for them, and re-layouts, sweep_blocks(): solved = solved.at[:, sweep_step_index].set(block_value)  41.6 us
  transfers between devices with their start and end apart: 25, of which 25 were waited for; matrix products, arithmetic and copies ran while one was open for 1% of the time, Pallas kernels for 0%

profile of v1, /device:TPU:0, one launch (start us, length us, event | category | flops | bytes accessed | tf_op | source)
XLA Modules:
  0.0 2004.6 jit_solution(5347846197804365636)
XLA Ops:
  18.0 73.5 %all-gather.49.cloned.1.call-done = f32[32,256,256]{2,1,0:T(8,128)} async-done(((f32[2,256,256]{2,1,0:T(8,128)}), f32[32,256,256]{2,1,0:T(8,128)}) %all-gather.49.cloned.1.call-update) | async-done | bytes 8388624 | tf_op jit(solution)/shard_map/all_gather | solution.py:31
  107.0 66.3 %all-gather.51.cloned.1.call-done = f32[32,256,256]{2,1,0:T(8,128)} async-done(((f32[2,256,256]{2,1,0:T(8,128)}), f32[32,256,256]{2,1,0:T(8,128)}) %all-gather.51.cloned.1.call-update) | async-done | bytes 8388624 | tf_op jit(solution)/shard_map/all_gather | solution.py:31
  187.5 70.6 %all-gather.53.cloned.1.call-done = f32[32,256,256]{2,1,0:T(8,128)} async-done(((f32[2,256,256]{2,1,0:T(8,128)}), f32[32,256,256]{2,1,0:T(8,128)}) %all-gather.53.cloned.1.call-update) | async-done | bytes 8388624 | tf_op jit(solution)/shard_map/all_gather | solution.py:31
  272.3 70.6 %all-gather.55.cloned.1.call-done = f32[32,256,256]{2,1,0:T(8,128)} async-done(((f32[2,256,256]{2,1,0:T(8,128)}), f32[32,256,256]{2,1,0:T(8,128)}) %all-gather.55.cloned.1.call-update) | async-done | bytes 8388624 | tf_op jit(solution)/shard_map/all_gather | solution.py:31
  357.6 70.2 %all-gather.57.cloned.1.call-done = f32[32,256,256]{2,1,0:T(8,128)} async-done(((f32[2,256,256]{2,1,0:T(8,128)}), f32[32,256,256]{2,1,0:T(8,128)}) %all-gather.57.cloned.1.call-update) | async-done | bytes 8388624 | tf_op jit(solution)/shard_map/all_gather | solution.py:31
  442.0 70.6 %all-gather.59.cloned.1.call-done = f32[32,256,256]{2,1,0:T(8,128)} async-done(((f32[2,256,256]{2,1,0:T(8,128)}), f32[32,256,256]{2,1,0:T(8,128)}) %all-gather.59.cloned.1.call-update) | async-done | bytes 8388624 | tf_op jit(solution)/shard_map/all_gather | solution.py:31
  526.8 70.6 %all-gather.61.cloned.1.call-done = f32[32,256,256]{2,1,0:T(8,128)} async-done(((f32[2,256,256]{2,1,0:T(8,128)}), f32[32,256,256]{2,1,0:T(8,128)}) %all-gather.61.cloned.1.call-update) | async-done | bytes 8388624 | tf_op jit(solution)/shard_map/all_gather | solution.py:31
  614.5 67.8 %all-gather.63.cloned.1.call-done = f32[32,256,256]{2,1,0:T(8,128)} async-done(((f32[2,256,256]{2,1,0:T(8,128)}), f32[32,256,256]{2,1,0:T(8,128)}) %all-gather.63.cloned.1.call-update) | async-done | bytes 8388624 | tf_op jit(solution)/shard_map/all_gather | solution.py:31
  754.7 56.3 %all-gather.65.cloned.1.call-done = f32[4096,256]{0,1:T(8,128)} async-done(((f32[256,256]{0,1:T(8,128)}), f32[4096,256]{0,1:T(8,128)}) %all-gather.65.cloned.1.call-update) | async-done | bytes 4194320 | tf_op jit(solution)/shard_map/all_gather | solution.py:31
  822.0 55.3 %all-gather.67.cloned.1.call-done = f32[4096,256]{0,1:T(8,128)} async-done(((f32[256,256]{0,1:T(8,128)}), f32[4096,256]{0,1:T(8,128)}) %all-gather.67.cloned.1.call-update) | async-done | bytes 4194320 | tf_op jit(solution)/shard_map/all_gather | solution.py:31
  888.0 56.3 %all-gather.69.cloned.1.call-done = f32[4096,256]{0,1:T(8,128)} async-done(((f32[256,256]{0,1:T(8,128)}), f32[4096,256]{0,1:T(8,128)}) %all-gather.69.cloned.1.call-update) | async-done | bytes 4194320 | tf_op jit(solution)/shard_map/all_gather | solution.py:31
  955.3 56.1 %all-gather.71.cloned.1.call-done = f32[4096,256]{0,1:T(8,128)} async-done(((f32[256,256]{0,1:T(8,128)}), f32[4096,256]{0,1:T(8,128)}) %all-gather.71.cloned.1.call-update) | async-done | bytes 4194320 | tf_op jit(solution)/shard_map/all_gather | solution.py:31
  1021.0 56.3 %all-gather.73.cloned.1.call-done = f32[4096,256]{0,1:T(8,128)} async-done(((f32[256,256]{0,1:T(8,128)}), f32[4096,256]{0,1:T(8,128)}) %all-gather.73.cloned.1.call-update) | async-done | bytes 4194320 | tf_op jit(solution)/shard_map/all_gather | solution.py:31
  1086.7 55.2 %all-gather.75.cloned.1.call-done = f32[4096,256]{0,1:T(8,128)} async-done(((f32[256,256]{0,1:T(8,128)}), f32[4096,256]{0,1:T(8,128)}) %all-gather.75.cloned.1.call-update) | async-done | bytes 4194320 | tf_op jit(solution)/shard_map/all_gather | solution.py:31
  1151.4 55.9 %all-gather.77.cloned.1.call-done = f32[4096,256]{0,1:T(8,128)} async-done(((f32[256,256]{0,1:T(8,128)}), f32[4096,256]{0,1:T(8,128)}) %all-gather.77.cloned.1.call-update) | async-done | bytes 4194320 | tf_op jit(solution)/shard_map/all_gather | solution.py:31
  1218.8 53.8 %all-gather.79.cloned.1.call-done = f32[4096,256]{0,1:T(8,128)} async-done(((f32[256,256]{0,1:T(8,128)}), f32[4096,256]{0,1:T(8,128)}) %all-gather.79.cloned.1.call-update) | async-done | bytes 4194320 | tf_op jit(solution)/shard_map/all_gather | solution.py:31
  1289.1 70.3 %all-gather.81.cloned.1.call-done = f32[32,256,256]{2,1,0:T(8,128)} async-done(((f32[2,256,256]{2,1,0:T(8,128)}), f32[32,256,256]{2,1,0:T(8,128)}) %all-gather.81.cloned.1.call-update) | async-done | bytes 8388624 | tf_op jit(solution)/shard_map/all_gather | solution.py:31
  1381.0 67.0 %all-gather.83.cloned.1.call-done = f32[32,256,256]{2,1,0:T(8,128)} async-done(((f32[2,256,256]{2,1,0:T(8,128)}), f32[32,256,256]{2,1,0:T(8,128)}) %all-gather.83.cloned.1.call-update) | async-done | bytes 8388624 | tf_op jit(solution)/shard_map/all_gather | solution.py:31
  1468.1 70.6 %all-gather.85.cloned.1.call-done = f32[32,256,256]{2,1,0:T(8,128)} async-done(((f32[2,256,256]{2,1,0:T(8,128)}), f32[32,256,256]{2,1,0:T(8,128)}) %all-gather.85.cloned.1.call-update) | async-done | bytes 8388624 | tf_op jit(solution)/shard_map/all_gather | solution.py:31
  1558.7 70.6 %all-gather.87.cloned.1.call-done = f32[32,256,256]{2,1,0:T(8,128)} async-done(((f32[2,256,256]{2,1,0:T(8,128)}), f32[32,256,256]{2,1,0:T(8,128)}) %all-gather.87.cloned.1.call-update) | async-done | bytes 8388624 | tf_op jit(solution)/shard_map/all_gather | solution.py:31
  1649.4 70.6 %all-gather.89.cloned.1.call-done = f32[32,256,256]{2,1,0:T(8,128)} async-done(((f32[2,256,256]{2,1,0:T(8,128)}), f32[32,256,256]{2,1,0:T(8,128)}) %all-gather.89.cloned.1.call-update) | async-done | bytes 8388624 | tf_op jit(solution)/shard_map/all_gather | solution.py:31
  1740.2 70.4 %all-gather.91.cloned.1.call-done = f32[32,256,256]{2,1,0:T(8,128)} async-done(((f32[2,256,256]{2,1,0:T(8,128)}), f32[32,256,256]{2,1,0:T(8,128)}) %all-gather.91.cloned.1.call-update) | async-done | bytes 8388624 | tf_op jit(solution)/shard_map/all_gather | solution.py:31
  1830.7 70.6 %all-gather.93.cloned.1.call-done = f32[32,256,256]{2,1,0:T(8,128)} async-done(((f32[2,256,256]{2,1,0:T(8,128)}), f32[32,256,256]{2,1,0:T(8,128)}) %all-gather.93.cloned.1.call-update) | async-done | bytes 8388624 | tf_op jit(solution)/shard_map/all_gather | solution.py:31
  1920.9 69.2 %all-gather.95.cloned.1.call-done = f32[32,256,256]{2,1,0:T(8,128)} async-done(((f32[2,256,256]{2,1,0:T(8,128)}), f32[32,256,256]{2,1,0:T(8,128)}) %all-gather.95.cloned.1.call-update) | async-done | bytes 8388624 | tf_op jit(solution)/shard_map/all_gather | solution.py:31
  (246 shorter events, 424.9 us)
Async XLA Ops:
  17.9 155.3 %all-gather.51.cloned.1.call-start = ((), (), s32[]{:S(2)}) async-start(), calls=%async_computation.2 | async-start | bytes 8912896 | tf_op jit(solution)/shard_map/all_gather | solution.py:31
  103.6 154.6 %all-gather.53.cloned.1.call-start = ((), (), s32[]{:S(2)}) async-start(), calls=%async_computation.3 | async-start | bytes 8912896 | tf_op jit(solution)/shard_map/all_gather | solution.py:31
  187.5 155.5 %all-gather.55.cloned.1.call-start = ((), (), s32[]{:S(2)}) async-start(), calls=%async_computation.4 | async-start | bytes 8912896 | tf_op jit(solution)/shard_map/all_gather | solution.py:31
  272.3 155.5 %all-gather.57.cloned.1.call-start = ((), (), s32[]{:S(2)}) async-start(), calls=%async_computation.5 | async-start | bytes 8912896 | tf_op jit(solution)/shard_map/all_gather | solution.py:31
  357.1 155.5 %all-gather.59.cloned.1.call-start = ((), (), s32[]{:S(2)}) async-start(), calls=%async_computation.6 | async-start | bytes 8912896 | tf_op jit(solution)/shard_map/all_gather | solution.py:31
  441.9 155.5 %all-gather.61.cloned.1.call-start = ((), (), s32[]{:S(2)}) async-start(), calls=%async_computation.7 | async-start | bytes 8912896 | tf_op jit(solution)/shard_map/all_gather | solution.py:31
  526.8 155.6 %all-gather.63.cloned.1.call-start = ((), (), s32[]{:S(2)}) async-start(), calls=%async_computation.8 | async-start | bytes 8912896 | tf_op jit(solution)/shard_map/all_gather | solution.py:31
  611.7 140.7 %all-reduce.6.cloned.1.call-start = ((), (), s32[]{:S(2)}) async-start(), calls=%async_computation | async-start | bytes 524288 | tf_op jit(solution)/shard_map/psum | solution.py:73
  692.4 118.6 %all-gather.65.cloned.1.call-start = ((), (), s32[]{:S(2)}) async-start(), calls=%async_computation.9 | async-start | bytes 4456448 | tf_op jit(solution)/shard_map/all_gather | solution.py:31
  754.4 122.8 %all-gather.67.cloned.1.call-start = ((), (), s32[]{:S(2)}) async-start(), calls=%async_computation.10 | async-start | bytes 4456448 | tf_op jit(solution)/shard_map/all_gather | solution.py:31
  820.9 123.4 %all-gather.69.cloned.1.call-start = ((), (), s32[]{:S(2)}) async-start(), calls=%async_computation.11 | async-start | bytes 4456448 | tf_op jit(solution)/shard_map/all_gather | solution.py:31
  888.0 123.4 %all-gather.71.cloned.1.call-start = ((), (), s32[]{:S(2)}) async-start(), calls=%async_computation.12 | async-start | bytes 4456448 | tf_op jit(solution)/shard_map/all_gather | solution.py:31
  955.1 122.3 %all-gather.73.cloned.1.call-start = ((), (), s32[]{:S(2)}) async-start(), calls=%async_computation.13 | async-start | bytes 4456448 | tf_op jit(solution)/shard_map/all_gather | solution.py:31
  1021.0 120.9 %all-gather.75.cloned.1.call-start = ((), (), s32[]{:S(2)}) async-start(), calls=%async_computation.14 | async-start | bytes 4456448 | tf_op jit(solution)/shard_map/all_gather | solution.py:31
  1085.5 121.8 %all-gather.77.cloned.1.call-start = ((), (), s32[]{:S(2)}) async-start(), calls=%async_computation.15 | async-start | bytes 4456448 | tf_op jit(solution)/shard_map/all_gather | solution.py:31
  1150.9 121.8 %all-gather.79.cloned.1.call-start = ((), (), s32[]{:S(2)}) async-start(), calls=%async_computation.16 | async-start | bytes 4456448 | tf_op jit(solution)/shard_map/all_gather | solution.py:31
  1216.3 143.1 %all-gather.81.cloned.1.call-start = ((), (), s32[]{:S(2)}) async-start(), calls=%async_computation.17 | async-start | bytes 8912896 | tf_op jit(solution)/shard_map/all_gather | solution.py:31
  1289.1 159.0 %all-gather.83.cloned.1.call-start = ((), (), s32[]{:S(2)}) async-start(), calls=%async_computation.18 | async-start | bytes 8912896 | tf_op jit(solution)/shard_map/all_gather | solution.py:31
  1377.4 161.3 %all-gather.85.cloned.1.call-start = ((), (), s32[]{:S(2)}) async-start(), calls=%async_computation.19 | async-start | bytes 8912896 | tf_op jit(solution)/shard_map/all_gather | solution.py:31
  1468.0 161.3 %all-gather.87.cloned.1.call-start = ((), (), s32[]{:S(2)}) async-start(), calls=%async_computation.20 | async-start | bytes 8912896 | tf_op jit(solution)/shard_map/all_gather | solution.py:31
  1558.7 161.3 %all-gather.89.cloned.1.call-start = ((), (), s32[]{:S(2)}) async-start(), calls=%async_computation.21 | async-start | bytes 8912896 | tf_op jit(solution)/shard_map/all_gather | solution.py:31
  1649.3 161.3 %all-gather.91.cloned.1.call-start = ((), (), s32[]{:S(2)}) async-start(), calls=%async_computation.22 | async-start | bytes 8912896 | tf_op jit(solution)/shard_map/all_gather | solution.py:31
  1740.0 161.3 %all-gather.93.cloned.1.call-start = ((), (), s32[]{:S(2)}) async-start(), calls=%async_computation.23 | async-start | bytes 8912896 | tf_op jit(solution)/shard_map/all_gather | solution.py:31
  1830.6 159.5 %all-gather.95.cloned.1.call-start = ((), (), s32[]{:S(2)}) async-start(), calls=%async_computation.24 | async-start | bytes 8912896 | tf_op jit(solution)/shard_map/all_gather | solution.py:31
  (9 other events, 1491.4 us)
Sparse Core Ops, SparseCore 0:
  18.1 73.4 all-gather.48
  103.7 69.5 all-gather.50
  187.6 70.5 all-gather.52
  272.4 70.5 all-gather.54
  357.2 70.5 all-gather.56
  442.1 70.5 all-gather.58
  526.9 70.4 all-gather.60
  611.8 70.5 all-gather.62
  692.5 59.7 all-reduce.5
  821.0 56.2 all-gather.66
  888.1 56.1 all-gather.68
  955.2 56.1 all-gather.70
  1021.1 56.1 all-gather.72
  1085.6 56.1 all-gather.74
  1151.0 56.2 all-gather.76
  1216.4 56.1 all-gather.78
  1289.2 70.1 all-gather.80
  1377.5 70.4 all-gather.82
  1468.2 70.4 all-gather.84
  1558.8 70.5 all-gather.86
  1649.5 70.5 all-gather.88
  1740.1 70.5 all-gather.90
  1830.7 70.4 all-gather.92
  1919.6 70.4 all-gather.94
  (1 shorter events, 56.0 us)
